TPU v7x, 128 devices: a whole 4x4x4 slice. The times are simulated.
128 devices in a mesh: dp: 16 (over x, z), tensor: 8 (over y, core).
Axes of the slice: x: 4, y: 4, z: 4, core: 2. Of those that a mesh axis runs over, the one named last changes fastest.
Arguments:
- attn_norm_grad: bfloat16 [16, 2048], P('dp', 'tensor'), may hold values from -1.5 to 1.5
- query_grad: bfloat16 [16, 2048, 2048], P('dp', None, 'tensor'), may hold values from -1.5 to 1.5
- forget_grad: bfloat16 [16, 2048, 2048], P('dp', None, 'tensor'), may hold values from -1.5 to 1.5
- input_grad: bfloat16 [16, 2048, 2048], P('dp', None, 'tensor'), may hold values from -1.5 to 1.5
- group_norm_grad: bfloat16 [16, 2048], P('dp', 'tensor'), may hold values from -1.5 to 1.5
- output_gate_grad: bfloat16 [16, 2048, 2048], P('dp', None, 'tensor'), may hold values from -1.5 to 1.5
- out_proj_grad: bfloat16 [16, 2048, 2048], P('dp', 'tensor'), may hold values from -1.5 to 1.5
- mlp_norm_grad: bfloat16 [16, 2048], P('dp', 'tensor'), may hold values from -1.5 to 1.5
- gate_proj_grad: bfloat16 [16, 2048, 2816], P('dp', None, 'tensor'), may hold values from -1.5 to 1.5
- up_proj_grad: bfloat16 [16, 2048, 2816], P('dp', None, 'tensor'), may hold values from -1.5 to 1.5
- down_proj_grad: bfloat16 [16, 2816, 2048], P('dp', 'tensor'), may hold values from -1.5 to 1.5
- weights: float32 [8, 4784896], P('tensor', 'dp'), as said below
- first_moment: float32 [8, 4784896], P('tensor', 'dp'), may hold values from -0.6 to 0.6
- second_moment: float32 [8, 4784896], P('tensor', 'dp'), may hold values from 0.001 to 1
Outputs:
- new_weights: float32 [8, 4784896], P('tensor', 'dp')
- new_first: float32 [8, 4784896], P('tensor', 'dp')
- new_second: float32 [8, 4784896], P('tensor', 'dp')
- attn_norm_copy: bfloat16 [2048], P('tensor')
- query_copy: bfloat16 [2048, 2048], P(None, 'tensor')
- forget_copy: bfloat16 [2048, 2048], P(None, 'tensor')
- input_copy: bfloat16 [2048, 2048], P(None, 'tensor')
- group_norm_copy: bfloat16 [2048], P('tensor')
- output_gate_copy: bfloat16 [2048, 2048], P(None, 'tensor')
- out_proj_copy: bfloat16 [2048, 2048], P('tensor')
- mlp_norm_copy: bfloat16 [2048], P('tensor')
- gate_proj_copy: bfloat16 [2048, 2816], P(None, 'tensor')
- up_proj_copy: bfloat16 [2048, 2816], P(None, 'tensor')
- down_proj_copy: bfloat16 [2816, 2048], P('tensor')
Inputs may be any that keep to these rules, and one draw needn't show every extreme that they name: float32 master weights of order one.
All inputs are finite; a program needn't handle non-finite values.
Results may differ from a plain program's by a relative error of at most 0.0085.
Values may be sent and summed in bfloat16 or wider, within the bound.
A program may use at most 192 MiB of HBM per device.

v0:
```python
import jax
import jax.numpy as jnp
from jax import lax
from jax.sharding import PartitionSpec as P

GAIN_SEGMENTS = (0, 4, 7)


def segment_sums(onehot, values):
    return jnp.dot(onehot, values, precision=lax.Precision.HIGHEST)


def split_rows(block, owners):
    if block.ndim == 1:
        return block.reshape(owners, block.shape[0] // owners)
    return block.reshape(owners, block.shape[0] // owners, block.shape[1])


def on_device(
    attn_norm_grad,
    query_grad,
    forget_grad,
    input_grad,
    group_norm_grad,
    output_gate_grad,
    out_proj_grad,
    mlp_norm_grad,
    gate_proj_grad,
    up_proj_grad,
    down_proj_grad,
    weights,
    first_moment,
    second_moment,
):
    grads = (
        attn_norm_grad,
        query_grad,
        forget_grad,
        input_grad,
        group_norm_grad,
        output_gate_grad,
        out_proj_grad,
        mlp_norm_grad,
        gate_proj_grad,
        up_proj_grad,
        down_proj_grad,
    )
    owners = lax.axis_size("dp")
    shapes = [g.shape[1:] for g in grads]
    pieces = [split_rows(g[0], owners) for g in grads]
    piece_len = [p[0].size for p in pieces]
    own_count = sum(piece_len)
    weight_row = weights.reshape(-1)
    first_row = first_moment.reshape(-1)
    second_row = second_moment.reshape(-1)
    position = jnp.arange(own_count, dtype=jnp.int32)
    segment = jnp.zeros((own_count,), jnp.int32)
    bound = 0
    for number in range(10):
        bound += piece_len[number]
        segment = segment + (position >= bound).astype(jnp.int32)
    onehot = (segment[None, :] == jnp.arange(11, dtype=jnp.int32)[:, None]).astype(jnp.float32)
    gain_mask = onehot[GAIN_SEGMENTS[0]] + onehot[GAIN_SEGMENTS[1]] + onehot[GAIN_SEGMENTS[2]]
    summed = (
        lax.psum_scatter(
            pieces[0].astype(jnp.float32).astype(jnp.bfloat16),
            "dp",
            scatter_dimension=0,
            tiled=True,
        ).astype(jnp.float32),
        lax.psum_scatter(
            pieces[1].astype(jnp.float32).astype(jnp.bfloat16),
            "dp",
            scatter_dimension=0,
            tiled=True,
        ).astype(jnp.float32),
        lax.psum_scatter(
            pieces[2].astype(jnp.float32).astype(jnp.bfloat16),
            "dp",
            scatter_dimension=0,
            tiled=True,
        ).astype(jnp.float32),
        lax.psum_scatter(
            pieces[3].astype(jnp.float32).astype(jnp.bfloat16),
            "dp",
            scatter_dimension=0,
            tiled=True,
        ).astype(jnp.float32),
        lax.psum_scatter(
            pieces[4].astype(jnp.float32).astype(jnp.bfloat16),
            "dp",
            scatter_dimension=0,
            tiled=True,
        ).astype(jnp.float32),
        lax.psum_scatter(
            pieces[5].astype(jnp.float32).astype(jnp.bfloat16),
            "dp",
            scatter_dimension=0,
            tiled=True,
        ).astype(jnp.float32),
        lax.psum_scatter(
            pieces[6].astype(jnp.float32).astype(jnp.bfloat16),
            "dp",
            scatter_dimension=0,
            tiled=True,
        ).astype(jnp.float32),
        lax.psum_scatter(
            pieces[7].astype(jnp.float32).astype(jnp.bfloat16),
            "dp",
            scatter_dimension=0,
            tiled=True,
        ).astype(jnp.float32),
        lax.psum_scatter(
            pieces[8].astype(jnp.float32).astype(jnp.bfloat16),
            "dp",
            scatter_dimension=0,
            tiled=True,
        ).astype(jnp.float32),
        lax.psum_scatter(
            pieces[9].astype(jnp.float32).astype(jnp.bfloat16),
            "dp",
            scatter_dimension=0,
            tiled=True,
        ).astype(jnp.float32),
        lax.psum_scatter(
            pieces[10].astype(jnp.float32).astype(jnp.bfloat16),
            "dp",
            scatter_dimension=0,
            tiled=True,
        ).astype(jnp.float32),
    )
    grad = jnp.concatenate([s.reshape(-1) for s in summed])
    new_first = 0.9 * first_row + 0.1 * grad
    new_second = 0.999 * second_row + 0.001 * grad * grad
    update = new_first / (jnp.sqrt(new_second) + 1e-06) + 0.01 * weight_row * (1.0 - gain_mask)
    weight_sq, update_sq = lax.psum(
        (segment_sums(onehot, weight_row * weight_row), segment_sums(onehot, update * update)),
        ("dp", "tensor"),
    )
    trust = jnp.sqrt(weight_sq) / jnp.sqrt(update_sq)
    scale = jnp.dot(trust, onehot, precision=lax.Precision.HIGHEST)
    new_weights = weight_row - 0.1 * scale * update
    rounded = new_weights.astype(jnp.bfloat16)
    owned = []
    offset = 0
    for number in range(11):
        owned.append(
            rounded[offset : offset + piece_len[number]].reshape((1,) + pieces[number].shape[1:])
        )
        offset += piece_len[number]
    gathered = (
        lax.all_gather(owned[0], "dp", axis=0, tiled=True),
        lax.all_gather(owned[1], "dp", axis=0, tiled=True),
        lax.all_gather(owned[2], "dp", axis=0, tiled=True),
        lax.all_gather(owned[3], "dp", axis=0, tiled=True),
        lax.all_gather(owned[4], "dp", axis=0, tiled=True),
        lax.all_gather(owned[5], "dp", axis=0, tiled=True),
        lax.all_gather(owned[6], "dp", axis=0, tiled=True),
        lax.all_gather(owned[7], "dp", axis=0, tiled=True),
        lax.all_gather(owned[8], "dp", axis=0, tiled=True),
        lax.all_gather(owned[9], "dp", axis=0, tiled=True),
        lax.all_gather(owned[10], "dp", axis=0, tiled=True),
    )
    copies = [gathered[number].reshape(shapes[number]) for number in range(11)]
    return (
        new_weights.reshape(1, -1),
        new_first.reshape(1, -1),
        new_second.reshape(1, -1),
        copies[0],
        copies[1],
        copies[2],
        copies[3],
        copies[4],
        copies[5],
        copies[6],
        copies[7],
        copies[8],
        copies[9],
        copies[10],
    )


def solution(mesh):
    return jax.shard_map(
        on_device,
        mesh=mesh,
        in_specs=(
            P("dp", "tensor"),
            P("dp", None, "tensor"),
            P("dp", None, "tensor"),
            P("dp", None, "tensor"),
            P("dp", "tensor"),
            P("dp", None, "tensor"),
            P("dp", "tensor", None),
            P("dp", "tensor"),
            P("dp", None, "tensor"),
            P("dp", None, "tensor"),
            P("dp", "tensor", None),
            P("tensor", "dp"),
            P("tensor", "dp"),
            P("tensor", "dp"),
        ),
        out_specs=(
            P("tensor", "dp"),
            P("tensor", "dp"),
            P("tensor", "dp"),
            P("tensor"),
            P(None, "tensor"),
            P(None, "tensor"),
            P(None, "tensor"),
            P("tensor"),
            P(None, "tensor"),
            P("tensor", None),
            P("tensor"),
            P(None, "tensor"),
            P(None, "tensor"),
            P("tensor", None),
        ),
        check_vma=False,
    )
```

profile of v0, /device:TPU:0, one launch (start us, length us, event | category | flops | bytes accessed | tf_op | source)
XLA Modules:
  0.0 1172.6 jit_solution(3635013927501478566)
XLA Ops:
  18.8 8.6 fusion.2
  27.7 13.4 %reduce = f32[299056]{0:T(1024)S(1)} reduce(f32[1,299056]{1,0:T(1,128)} %param.25, f32[]{:T(128)} %constant.110), dimensions={0}, to_apply=%param.25.reduce_sub_computation | reduce | bytes 2392452 | tf_op args[11]
  41.1 76.1 %all-reduce.16 = (bf16[16,16]{1,0:T(8,128)(2,1)S(1)}, bf16[16,16]{1,0:T(8,128)(2,1)S(1)}, bf16[16,16]{1,0:T(8,128)(2,1)S(1)}) all-reduce(bf16[16,16]{1,0:T(8,128)(2,1)S(1)} %reshape_squeeze.33, bf16[16,16]{1,0:T(8,128)(2,1)S(1)} %reshape_squeeze.37, ...), channel_id=5, replica_groups=mesh['dp'=16,'tensor'=8] {'dp'}, use_global_device_ids=true, to_apply=%region_1.0.clone | all-reduce | flops 768 | bytes 3072
  121.0 20.0 %fusion.15 = f32[299056]{0:T(1024)} fusion(f32[11,299056]{1,0:T(8,128)} %fusion.2), kind=kLoop, calls=%fused_computation.35 | loop fusion | flops 897168 | bytes 4784896 | tf_op jit(solution)/shard_map/sub | solution.py:135
  142.1 20.7 %reduce-scatter.27.cloned.1.call-done = bf16[1,128,256]{2,1,0:T(8,128)(2,1)} async-done(((bf16[16,128,256]{2,1,0:T(8,128)(2,1)}), bf16[1,128,256]{2,1,0:T(8,128)(2,1)}) %reduce-scatter.27.cloned.1.call-update) | async-done | bytes 65552
  163.7 74.5 %reduce-scatter.29.cloned.1.call-done = bf16[1,128,256]{2,1,0:T(8,128)(2,1)} async-done(((bf16[16,128,256]{2,1,0:T(8,128)(2,1)}), bf16[1,128,256]{2,1,0:T(8,128)(2,1)}) %reduce-scatter.29.cloned.1.call-update) | async-done | bytes 65552
  239.9 74.0 %reduce-scatter.31.cloned.1.call-done = bf16[1,128,256]{2,1,0:T(8,128)(2,1)} async-done(((bf16[16,128,256]{2,1,0:T(8,128)(2,1)}), bf16[1,128,256]{2,1,0:T(8,128)(2,1)}) %reduce-scatter.31.cloned.1.call-update) | async-done | bytes 65552
  315.6 73.7 %reduce-scatter.33.cloned.1.call-done = bf16[1,16,2048]{2,1,0:T(8,128)(2,1)} async-done(((bf16[16,16,2048]{2,1,0:T(8,128)(2,1)}), bf16[1,16,2048]{2,1,0:T(8,128)(2,1)}) %reduce-scatter.33.cloned.1.call-update) | async-done | bytes 65552
  414.8 51.4 %reduce-scatter.35.cloned.1.call-done = bf16[1,128,352]{1,2,0:T(8,128)(2,1)} async-done(((bf16[16,128,352]{1,2,0:T(8,128)(2,1)}), bf16[1,128,352]{1,2,0:T(8,128)(2,1)}) %reduce-scatter.35.cloned.1.call-update) | async-done | bytes 90128
  467.7 75.6 %reduce-scatter.37.cloned.1.call-done = bf16[1,128,352]{1,2,0:T(8,128)(2,1)} async-done(((bf16[16,128,352]{1,2,0:T(8,128)(2,1)}), bf16[1,128,352]{1,2,0:T(8,128)(2,1)}) %reduce-scatter.37.cloned.1.call-update) | async-done | bytes 90128
  544.8 75.0 %reduce-scatter.39.cloned.1.call-done = bf16[1,22,2048]{2,1,0:T(8,128)(2,1)} async-done(((bf16[16,22,2048]{2,1,0:T(8,128)(2,1)}), bf16[1,22,2048]{2,1,0:T(8,128)(2,1)}) %reduce-scatter.39.cloned.1.call-update) | async-done | bytes 90128
  620.9 4.4 dynamic-update-slice.11
  625.3 4.4 dynamic-update-slice.12
  629.6 4.3 dynamic-update-slice.13
  634.0 21.6 %fusion.13 = (f32[1,299056]{1,0:T(1,128)}, f32[299056]{0:T(1024)}, f32[1,299056]{1,0:T(1,128)}, f32[299056]{0:T(1024)}) fusion(f32[1,299056]{1,0:T(1,128)} %dynamic-update-slice.13, f32[1,299056]{1,0:T(1,128)} %param.27, f32[1,299056]{1,0:T(1,128)} %param.26), kind=kLoop, calls=%fused_computation.30 | loop fusion | flops 2093392 | bytes 8373568 | tf_op jit(solution)/shard_map/add | solution.py:134
  655.7 16.2 %concatenate.41 = f32[299056]{0:T(1024)} concatenate(f32[16]{0:T(128)S(1)} %bitcast.103, f32[32768]{0:T(1024)S(1)} %bitcast.93, f32[32768]{0:T(1024)S(1)} %bitcast.94, f32[32768]{0:T(1024)S(1)} %bitcast.95, f32[16]{0:T(128)S(1)} %fusion.32, f32[32768]{0:T(1024)} %bitcast.96, f32[32768]{0:T(1024)} %bitcast.97, f32[16]{0:T(128)S(1)} %bitcast.104, f32[45056]{0:T(1024)S(1)} %reshape.617, ...), dimensions={0} | concatenate | bytes 2392448 | tf_op jit(solution)/shard_map/concatenate | solution.py:132
  671.9 4.2 fusion.24
  676.1 5.7 reshape.666
  681.8 12.5 %fusion.17 = f32[11]{0:T(128)S(1)} fusion(f32[299056,1]{0,1:T(1,128)S(1)} %reshape.666, s32[299056]{0:T(1024)S(1)} %convert_add_fusion), kind=kOutput, calls=%fused_computation.37 | convolution fusion | flops 42765008 | bytes 2392492 | tf_op jit(solution)/shard_map/dot_general | solution.py:10
  694.3 5.8 reshape.664
  700.1 12.5 %fusion.16 = f32[11]{0:T(128)S(1)} fusion(f32[299056,1]{0,1:T(1,128)S(1)} %reshape.664, s32[299056]{0:T(1024)S(1)} %convert_add_fusion), kind=kOutput, calls=%fused_computation.36 | convolution fusion | flops 42765008 | bytes 2392492 | tf_op jit(solution)/shard_map/dot_general | solution.py:10
  712.6 65.0 %all-reduce.14 = (f32[11]{0:T(128)S(1)}, f32[11]{0:T(128)S(1)}) all-reduce(f32[11]{0:T(128)S(1)} %fusion.17, f32[11]{0:T(128)S(1)} %fusion.16), channel_id=1, replica_groups=mesh['dp'=16,'tensor'=8] {'dp','tensor'}, use_global_device_ids=true, to_apply=%region_12.0 | all-reduce | flops 22 | bytes 176 | tf_op jit(solution)/shard_map/psum | solution.py:136
  777.6 20.0 %fusion.7 = f32[299056]{0:T(1024)S(1)} fusion(s32[299056]{0:T(1024)S(1)} %convert_add_fusion, f32[11]{0:T(128)S(1)} %get-tuple-element.28, f32[11]{0:T(128)S(1)} %get-tuple-element.29), kind=kOutput, calls=%fused_computation.22 | convolution fusion | flops 42765020 | bytes 2392536 | tf_op jit(solution)/shard_map/dot_general | solution.py:141
  805.2 6.5 reshape.620
  812.4 38.4 %all-reduce.15 = (bf16[256]{0:T(256)(128)(2,1)}, bf16[256]{0:T(256)(128)(2,1)}, bf16[256]{0:T(256)(128)(2,1)}) all-reduce(bf16[256]{0:T(256)(128)(2,1)S(1)} %dynamic-update-slice, bf16[256]{0:T(256)(128)(2,1)S(1)} %dynamic-update-slice.1, bf16[256]{0:T(256)(128)(2,1)S(1)} %dynamic-update-slice.2), channel_id=2, replica_groups=mesh['dp'=16,'tensor'=8] {'dp'}, use_global_device_ids=true, to_apply=%add | all-reduce | flops 768 | bytes 3072
  850.8 31.7 %all-gather.14.cloned.1.call-done = bf16[16,128,256]{2,1,0:T(8,128)(2,1)} async-done(((bf16[1,128,256]{2,1,0:T(8,128)(2,1)}), bf16[16,128,256]{2,1,0:T(8,128)(2,1)}) %all-gather.14.cloned.1.call-update) | async-done | bytes 1048592 | tf_op jit(solution)/shard_map/all_gather | solution.py:154
  882.5 45.1 %all-gather.16.cloned.1.call-done = bf16[16,128,256]{2,1,0:T(8,128)(2,1)} async-done(((bf16[1,128,256]{2,1,0:T(8,128)(2,1)}), bf16[16,128,256]{2,1,0:T(8,128)(2,1)}) %all-gather.16.cloned.1.call-update) | async-done | bytes 1048592 | tf_op jit(solution)/shard_map/all_gather | solution.py:155
  927.6 44.9 %all-gather.18.cloned.1.call-done = bf16[16,128,256]{2,1,0:T(8,128)(2,1)} async-done(((bf16[1,128,256]{2,1,0:T(8,128)(2,1)}), bf16[16,128,256]{2,1,0:T(8,128)(2,1)}) %all-gather.18.cloned.1.call-update) | async-done | bytes 1048592 | tf_op jit(solution)/shard_map/all_gather | solution.py:157
  972.5 45.1 %all-gather.20.cloned.1.call-done = bf16[16,16,2048]{2,1,0:T(8,128)(2,1)} async-done(((bf16[1,16,2048]{2,1,0:T(8,128)(2,1)}), bf16[16,16,2048]{2,1,0:T(8,128)(2,1)}) %all-gather.20.cloned.1.call-update) | async-done | bytes 1048592 | tf_op jit(solution)/shard_map/all_gather | solution.py:158
  1017.6 46.1 %all-gather.22.cloned.1.call-done = bf16[16,128,352]{1,2,0:T(8,128)(2,1)} async-done(((bf16[1,128,352]{1,2,0:T(8,128)(2,1)}), bf16[16,128,352]{1,2,0:T(8,128)(2,1)}) %all-gather.22.cloned.1.call-update) | async-done | bytes 1441808 | tf_op jit(solution)/shard_map/all_gather | solution.py:160
  1066.3 43.5 %all-gather.24.cloned.1.call-done = bf16[16,128,352]{1,2,0:T(8,128)(2,1)} async-done(((bf16[1,128,352]{1,2,0:T(8,128)(2,1)}), bf16[16,128,352]{1,2,0:T(8,128)(2,1)}) %all-gather.24.cloned.1.call-update) | async-done | bytes 1441808 | tf_op jit(solution)/shard_map/all_gather | solution.py:161
  1112.4 43.6 %all-gather.26.cloned.1.call-done = bf16[16,22,2048]{2,1,0:T(8,128)(2,1)} async-done(((bf16[1,22,2048]{2,1,0:T(8,128)(2,1)}), bf16[16,22,2048]{2,1,0:T(8,128)(2,1)}) %all-gather.26.cloned.1.call-update) | async-done | bytes 1441808 | tf_op jit(solution)/shard_map/all_gather | solution.py:162
  (147 shorter events, 72.9 us)
Async XLA Ops:
  7.2 133.9 %reduce-scatter.25.cloned.1.call-start = ((), (), s32[]{:S(2)}) async-start(), calls=%async_computation.16 | async-start | bytes 1114112
  7.9 154.8 %reduce-scatter.27.cloned.1.call-start = ((), (), s32[]{:S(2)}) async-start(), calls=%async_computation.17 | async-start | bytes 1114112
  8.7 229.6 %reduce-scatter.29.cloned.1.call-start = ((), (), s32[]{:S(2)}) async-start(), calls=%async_computation.18 | async-start | bytes 1114112
  9.4 1.4 copy-start.1
  9.4 304.5 %reduce-scatter.31.cloned.1.call-start = ((), (), s32[]{:S(2)}) async-start(), calls=%async_computation.19 | async-start | bytes 1114112
  10.0 379.3 %reduce-scatter.33.cloned.1.call-start = ((), (), s32[]{:S(2)}) async-start(), calls=%async_computation.20 | async-start | bytes 1114112
  10.6 455.7 %reduce-scatter.35.cloned.1.call-start = ((), (), s32[]{:S(2)}) async-start(), calls=%async_computation.21 | async-start | bytes 1531904
  12.6 530.7 %reduce-scatter.37.cloned.1.call-start = ((), (), s32[]{:S(2)}) async-start(), calls=%async_computation.22 | async-start | bytes 1531904
  15.8 604.0 %reduce-scatter.39.cloned.1.call-start = ((), (), s32[]{:S(2)}) async-start(), calls=%async_computation.23 | async-start | bytes 1671168
  18.6 832.3 %all-gather.12.cloned.1.call-start = ((), (), s32[]{:S(2)}) async-start(), calls=%async_computation.8 | async-start | bytes 1114112 | tf_op jit(solution)/shard_map/all_gather | solution.py:153
  18.7 8.6 copy-start.15
  18.7 8.7 copy-start.16
  18.7 8.8 copy-start.17
  27.7 89.5 %copy-start.14 = (u32[128]{0:T(128)S(1)}, u32[128]{0:T(128)}, u32[]{:S(2)}) copy-start(u32[128]{0:T(128)} %constant.50) | copy-start | bytes 1540
  389.3 1.9 copy-start.11
  389.3 2.6 copy-start.12
  633.9 21.6 %copy-start.13 = (bf16[1,22,2048]{2,1,0:T(8,128)(2,1)S(1)}, bf16[1,22,2048]{2,1,0:T(8,128)(2,1)}, u32[]{:S(2)}) copy-start(bf16[1,22,2048]{2,1,0:T(8,128)(2,1)} %reduce-scatter.39.cloned.1.call-done) | copy-start | bytes 270340
  633.9 21.7 %copy-start.9 = (f32[16,2,8,128]{3,1,2,0:T(2,128)S(1)}, f32[16,2,8,128]{3,1,2,0:T(2,128)}, u32[]{:S(2)}) copy-start(f32[16,2,8,128]{3,1,2,0:T(2,128)} %copy.53) | copy-start | bytes 393220
  634.0 21.7 %copy-start.10 = (f32[16,2,8,128]{3,1,2,0:T(2,128)S(1)}, f32[16,2,8,128]{3,1,2,0:T(2,128)}, u32[]{:S(2)}) copy-start(f32[16,2,8,128]{3,1,2,0:T(2,128)} %copy.54) | copy-start | bytes 393220
  777.6 20.0 %copy-start = (f32[299056]{0:T(1024)S(1)}, f32[299056]{0:T(1024)}, u32[]{:S(2)}) copy-start(f32[299056]{0:T(1024)} %get-tuple-element.39) | copy-start | bytes 3588676
  798.7 83.8 %all-gather.14.cloned.1.call-start = ((), (), s32[]{:S(2)}) async-start(), calls=%async_computation.9 | async-start | bytes 1114112 | tf_op jit(solution)/shard_map/all_gather | solution.py:154
  799.5 128.2 %all-gather.16.cloned.1.call-start = ((), (), s32[]{:S(2)}) async-start(), calls=%async_computation.10 | async-start | bytes 1114112 | tf_op jit(solution)/shard_map/all_gather | solution.py:155
  800.2 172.3 %all-gather.18.cloned.1.call-start = ((), (), s32[]{:S(2)}) async-start(), calls=%async_computation.11 | async-start | bytes 1114112 | tf_op jit(solution)/shard_map/all_gather | solution.py:157
  800.9 216.7 %all-gather.20.cloned.1.call-start = ((), (), s32[]{:S(2)}) async-start(), calls=%async_computation.12 | async-start | bytes 1114112 | tf_op jit(solution)/shard_map/all_gather | solution.py:158
  801.7 262.0 %all-gather.22.cloned.1.call-start = ((), (), s32[]{:S(2)}) async-start(), calls=%async_computation.13 | async-start | bytes 1531904 | tf_op jit(solution)/shard_map/all_gather | solution.py:160
  802.8 307.0 %all-gather.24.cloned.1.call-start = ((), (), s32[]{:S(2)}) async-start(), calls=%async_computation.14 | async-start | bytes 1531904 | tf_op jit(solution)/shard_map/all_gather | solution.py:161
  803.8 352.2 %all-gather.26.cloned.1.call-start = ((), (), s32[]{:S(2)}) async-start(), calls=%async_computation.15 | async-start | bytes 1671168 | tf_op jit(solution)/shard_map/all_gather | solution.py:162
  1112.4 46.0 %copy-start.4 = (bf16[16,128,256]{2,1,0:T(8,128)(2,1)S(1)}, bf16[16,128,256]{2,1,0:T(8,128)(2,1)}, u32[]{:S(2)}) copy-start(bf16[16,128,256]{2,1,0:T(8,128)(2,1)} %all-gather.12.cloned.1.call-done) | copy-start | bytes 3145732
  1158.5 1.6 copy-start.5
  1160.1 1.6 copy-start.6
  1161.7 1.6 copy-start.7
  1163.3 1.6 copy-start.8
  (2 other events, 2.7 us)
Sparse Core Ops, SparseCore 0:
  11.2 75.6 reduce-scatter.24
  90.4 72.2 reduce-scatter.26
  165.9 72.2 reduce-scatter.28
  241.7 72.2 reduce-scatter.30
  317.0 72.2 reduce-scatter.32
  393.3 72.8 reduce-scatter.34
  470.4 72.9 reduce-scatter.36
  546.9 72.9 reduce-scatter.38
  798.8 38.8 all-gather.11
  840.6 41.9 all-gather.13
  885.5 42.0 all-gather.15
  930.4 42.0 all-gather.17
  975.5 42.0 all-gather.19
  1020.5 43.1 all-gather.21
  1066.5 43.2 all-gather.23
  1112.6 43.3 all-gather.25
where the time goes:
time: 1180 us; the launch traced here: 1170 us
  waiting for transfers between devices  748 us (63%)
  blocking collectives  180 us (15%)
  local copies, waits for them, and re-layouts  107 us (9%)
  other arithmetic  76.6 us (6%)
  matrix products  45 us (4%)
  between operations  15.1 us (1%)
    unnamed x24, waiting for transfers between devices  448 us
    unnamed x2, blocking collectives  115 us
    psum x1, blocking collectives, on_device(): lax.psum((segment_sums(onehot, weight_row * weight_row), segment_sums(one...  65 us
    unnamed x71, local copies, waits for them, and re-layouts  47.3 us
    all_gather x1, waiting for transfers between devices, on_device(): lax.all_gather(owned[8], 'dp', axis=0, tiled=True)  46.1 us
    all_gather x1, waiting for transfers between devices, on_device(): lax.all_gather(owned[3], 'dp', axis=0, tiled=True)  45.1 us
    all_gather x1, waiting for transfers between devices, on_device(): lax.all_gather(owned[6], 'dp', axis=0, tiled=True)  45.1 us
    all_gather x1, waiting for transfers between devices, on_device(): lax.all_gather(owned[5], 'dp', axis=0, tiled=True)  44.9 us
  transfers between devices with their start and end apart: 16, of which 14 were waited for; matrix products, arithmetic and copies ran while one was open for 9% of the time, Pallas kernels for 0%

commit v1 on v0

--- a/solution.py
+++ b/solution.py
@@ -1,9 +1,22 @@
+import functools
 import jax
 import jax.numpy as jnp
 from jax import lax
 from jax.sharding import PartitionSpec as P
 
 GAIN_SEGMENTS = (0, 4, 7)
+
+
+def proceed_sectors(here_x, axis_key, array_dim):
+    runs = []
+    for _ in range(lax.psum(1, axis_name=axis_key)):
+        runs.append(here_x)
+    y1 = jnp.stack(runs, axis=0)
+    upper = lax.all_to_all(y1, split_axis=0, axis_name=axis_key, concat_axis=0)
+    return jnp.concatenate(upper, axis=array_dim)
+
+
+group_records = functools.partial(proceed_sectors, axis_key="dp", array_dim=0)
 
 
 def segment_sums(onehot, values):
@@ -151,7 +164,7 @@
     gathered = (
         lax.all_gather(owned[0], "dp", axis=0, tiled=True),
         lax.all_gather(owned[1], "dp", axis=0, tiled=True),
-        lax.all_gather(owned[2], "dp", axis=0, tiled=True),
+        group_records(owned[2]),
         lax.all_gather(owned[3], "dp", axis=0, tiled=True),
         lax.all_gather(owned[4], "dp", axis=0, tiled=True),
         lax.all_gather(owned[5], "dp", axis=0, tiled=True),

time: 1180 us -> 1140 us (0.966)
  waiting for transfers between devices: 748 us -> 703 us
    all_gather x1 -> x0, waiting for transfers between devices: 31.7 us -> none  [on_device(): lax.all_gather(owned[2], 'dp', axis=0, tiled=True)]
    all_gather x1, waiting for transfers between devices: 45.1 us -> 30.8 us  [on_device(): lax.all_gather(owned[3], 'dp', axis=0, tiled=True)]
    unnamed x71 -> x69, local copies, waits for them, and re-layouts: 47.3 us -> 46.7 us
    unnamed x24 -> x23, waiting for transfers between devices: 448 us -> 449 us
  transfers between devices with their start and end apart: 16 -> 16, of which waited for: 14 -> 13; matrix products, arithmetic and copies ran while one was open for 9% -> 9% of each run, Pallas kernels for 0% -> 0%
where the time goes in v1:
time: 1140 us; the launch traced here: 1130 us
  waiting for transfers between devices  703 us (62%)
  blocking collectives  182 us (16%)
  local copies, waits for them, and re-layouts  107 us (9%)
  other arithmetic  76.6 us (7%)
  matrix products  45 us (4%)
  between operations  15.1 us (1%)
    unnamed x23, waiting for transfers between devices  449 us
    unnamed x2, blocking collectives  117 us
    psum x1, blocking collectives, on_device(): lax.psum((segment_sums(onehot, weight_row * weight_row), segment_sums(one...  65 us
    unnamed x69, local copies, waits for them, and re-layouts  46.7 us
    all_gather x1, waiting for transfers between devices, on_device(): lax.all_gather(owned[8], 'dp', axis=0, tiled=True)  46.2 us
    all_gather x1, waiting for transfers between devices, on_device(): lax.all_gather(owned[5], 'dp', axis=0, tiled=True)  45.1 us
    all_gather x1, waiting for transfers between devices, on_device(): lax.all_gather(owned[6], 'dp', axis=0, tiled=True)  44.9 us
    all_gather x1, waiting for transfers between devices, on_device(): lax.all_gather(owned[10], 'dp', axis=0, tiled=True)  43.6 us
  transfers between devices with their start and end apart: 16, of which 13 were waited for; matrix products, arithmetic and copies ran while one was open for 9% of the time, Pallas kernels for 0%

profile of v1, /device:TPU:0, one launch (start us, length us, event | category | flops | bytes accessed | tf_op | source)
XLA Modules:
  0.0 1133.1 jit_solution(16901356541520015950)
XLA Ops:
  18.7 8.6 fusion.2
  27.7 13.4 %reduce = f32[299056]{0:T(1024)S(1)} reduce(f32[1,299056]{1,0:T(1,128)} %param.25, f32[]{:T(128)} %constant.110), dimensions={0}, to_apply=%param.25.reduce_sub_computation | reduce | bytes 2392452 | tf_op args[11]
  41.0 76.2 %all-reduce.16 = (bf16[16,16]{1,0:T(8,128)(2,1)S(1)}, bf16[16,16]{1,0:T(8,128)(2,1)S(1)}, bf16[16,16]{1,0:T(8,128)(2,1)S(1)}) all-reduce(bf16[16,16]{1,0:T(8,128)(2,1)S(1)} %reshape_squeeze.33, bf16[16,16]{1,0:T(8,128)(2,1)S(1)} %reshape_squeeze.37, ...), channel_id=5, replica_groups=mesh['dp'=16,'tensor'=8] {'dp'}, use_global_device_ids=true, to_apply=%region_1.0.clone | all-reduce | flops 768 | bytes 3072
  121.0 20.0 %fusion.15 = f32[299056]{0:T(1024)} fusion(f32[11,299056]{1,0:T(8,128)} %fusion.2), kind=kLoop, calls=%fused_computation.35 | loop fusion | flops 897168 | bytes 4784896 | tf_op jit(solution)/shard_map/sub | solution.py:148
  142.0 20.7 %reduce-scatter.27.cloned.1.call-done = bf16[1,128,256]{2,1,0:T(8,128)(2,1)} async-done(((bf16[16,128,256]{2,1,0:T(8,128)(2,1)}), bf16[1,128,256]{2,1,0:T(8,128)(2,1)}) %reduce-scatter.27.cloned.1.call-update) | async-done | bytes 65552
  163.8 74.6 %reduce-scatter.29.cloned.1.call-done = bf16[1,128,256]{2,1,0:T(8,128)(2,1)} async-done(((bf16[16,128,256]{2,1,0:T(8,128)(2,1)}), bf16[1,128,256]{2,1,0:T(8,128)(2,1)}) %reduce-scatter.29.cloned.1.call-update) | async-done | bytes 65552
  240.0 74.0 %reduce-scatter.31.cloned.1.call-done = bf16[1,128,256]{2,1,0:T(8,128)(2,1)} async-done(((bf16[16,128,256]{2,1,0:T(8,128)(2,1)}), bf16[1,128,256]{2,1,0:T(8,128)(2,1)}) %reduce-scatter.31.cloned.1.call-update) | async-done | bytes 65552
  315.7 73.7 %reduce-scatter.33.cloned.1.call-done = bf16[1,16,2048]{2,1,0:T(8,128)(2,1)} async-done(((bf16[16,16,2048]{2,1,0:T(8,128)(2,1)}), bf16[1,16,2048]{2,1,0:T(8,128)(2,1)}) %reduce-scatter.33.cloned.1.call-update) | async-done | bytes 65552
  414.9 51.5 %reduce-scatter.35.cloned.1.call-done = bf16[1,128,352]{1,2,0:T(8,128)(2,1)} async-done(((bf16[16,128,352]{1,2,0:T(8,128)(2,1)}), bf16[1,128,352]{1,2,0:T(8,128)(2,1)}) %reduce-scatter.35.cloned.1.call-update) | async-done | bytes 90128
  467.8 75.6 %reduce-scatter.37.cloned.1.call-done = bf16[1,128,352]{1,2,0:T(8,128)(2,1)} async-done(((bf16[16,128,352]{1,2,0:T(8,128)(2,1)}), bf16[1,128,352]{1,2,0:T(8,128)(2,1)}) %reduce-scatter.37.cloned.1.call-update) | async-done | bytes 90128
  544.9 75.2 %reduce-scatter.39.cloned.1.call-done = bf16[1,22,2048]{2,1,0:T(8,128)(2,1)} async-done(((bf16[16,22,2048]{2,1,0:T(8,128)(2,1)}), bf16[1,22,2048]{2,1,0:T(8,128)(2,1)}) %reduce-scatter.39.cloned.1.call-update) | async-done | bytes 90128
  621.1 4.4 dynamic-update-slice.11
  625.5 4.4 dynamic-update-slice.12
  629.8 4.3 dynamic-update-slice.13
  634.2 21.6 %fusion.13 = (f32[1,299056]{1,0:T(1,128)}, f32[299056]{0:T(1024)}, f32[1,299056]{1,0:T(1,128)}, f32[299056]{0:T(1024)}) fusion(f32[1,299056]{1,0:T(1,128)} %dynamic-update-slice.13, f32[1,299056]{1,0:T(1,128)} %param.27, f32[1,299056]{1,0:T(1,128)} %param.26), kind=kLoop, calls=%fused_computation.30 | loop fusion | flops 2093392 | bytes 8373568 | tf_op jit(solution)/shard_map/add | solution.py:147
  655.9 16.2 %concatenate.41 = f32[299056]{0:T(1024)} concatenate(f32[16]{0:T(128)S(1)} %bitcast.103, f32[32768]{0:T(1024)S(1)} %bitcast.93, f32[32768]{0:T(1024)S(1)} %bitcast.94, f32[32768]{0:T(1024)S(1)} %bitcast.95, f32[16]{0:T(128)S(1)} %fusion.32, f32[32768]{0:T(1024)} %bitcast.96, f32[32768]{0:T(1024)} %bitcast.97, f32[16]{0:T(128)S(1)} %bitcast.104, f32[45056]{0:T(1024)S(1)} %reshape.615, ...), dimensions={0} | concatenate | bytes 2392448 | tf_op jit(solution)/shard_map/concatenate | solution.py:145
  672.1 4.2 fusion.24
  676.3 5.7 reshape.662
  682.0 12.5 %fusion.17 = f32[11]{0:T(128)S(1)} fusion(f32[299056,1]{0,1:T(1,128)S(1)} %reshape.662, s32[299056]{0:T(1024)S(1)} %convert_add_fusion), kind=kOutput, calls=%fused_computation.37 | convolution fusion | flops 42765008 | bytes 2392492 | tf_op jit(solution)/shard_map/dot_general | solution.py:23
  694.5 5.8 reshape.660
  700.3 12.5 %fusion.16 = f32[11]{0:T(128)S(1)} fusion(f32[299056,1]{0,1:T(1,128)S(1)} %reshape.660, s32[299056]{0:T(1024)S(1)} %convert_add_fusion), kind=kOutput, calls=%fused_computation.36 | convolution fusion | flops 42765008 | bytes 2392492 | tf_op jit(solution)/shard_map/dot_general | solution.py:23
  712.8 65.0 %all-reduce.14 = (f32[11]{0:T(128)S(1)}, f32[11]{0:T(128)S(1)}) all-reduce(f32[11]{0:T(128)S(1)} %fusion.17, f32[11]{0:T(128)S(1)} %fusion.16), channel_id=1, replica_groups=mesh['dp'=16,'tensor'=8] {'dp','tensor'}, use_global_device_ids=true, to_apply=%region_12.0 | all-reduce | flops 22 | bytes 176 | tf_op jit(solution)/shard_map/psum | solution.py:149
  777.8 20.0 %fusion.7 = f32[299056]{0:T(1024)S(1)} fusion(s32[299056]{0:T(1024)S(1)} %convert_add_fusion, f32[11]{0:T(128)S(1)} %get-tuple-element.28, f32[11]{0:T(128)S(1)} %get-tuple-element.29), kind=kOutput, calls=%fused_computation.22 | convolution fusion | flops 42765020 | bytes 2392536 | tf_op jit(solution)/shard_map/dot_general | solution.py:154
  805.1 3.8 all-to-all-start
  809.6 6.3 reshape.618
  816.6 41.1 %all-reduce.15 = (bf16[256]{0:T(256)(128)(2,1)}, bf16[256]{0:T(256)(128)(2,1)}, bf16[256]{0:T(256)(128)(2,1)}) all-reduce(bf16[256]{0:T(256)(128)(2,1)S(1)} %dynamic-update-slice, bf16[256]{0:T(256)(128)(2,1)S(1)} %dynamic-update-slice.1, bf16[256]{0:T(256)(128)(2,1)S(1)} %dynamic-update-slice.2), channel_id=2, replica_groups=mesh['dp'=16,'tensor'=8] {'dp'}, use_global_device_ids=true, to_apply=%add | all-reduce | flops 768 | bytes 3072
  857.8 30.8 %all-gather.13.cloned.1.call-done = bf16[16,128,256]{2,1,0:T(8,128)(2,1)} async-done(((bf16[1,128,256]{2,1,0:T(8,128)(2,1)}), bf16[16,128,256]{2,1,0:T(8,128)(2,1)}) %all-gather.13.cloned.1.call-update) | async-done | bytes 1048592 | tf_op jit(solution)/shard_map/all_gather | solution.py:168
  888.6 45.1 %all-gather.15.cloned.1.call-done = bf16[16,128,256]{2,1,0:T(8,128)(2,1)} async-done(((bf16[1,128,256]{2,1,0:T(8,128)(2,1)}), bf16[16,128,256]{2,1,0:T(8,128)(2,1)}) %all-gather.15.cloned.1.call-update) | async-done | bytes 1048592 | tf_op jit(solution)/shard_map/all_gather | solution.py:170
  933.7 44.9 %all-gather.17.cloned.1.call-done = bf16[16,16,2048]{2,1,0:T(8,128)(2,1)} async-done(((bf16[1,16,2048]{2,1,0:T(8,128)(2,1)}), bf16[16,16,2048]{2,1,0:T(8,128)(2,1)}) %all-gather.17.cloned.1.call-update) | async-done | bytes 1048592 | tf_op jit(solution)/shard_map/all_gather | solution.py:171
  978.6 46.2 %all-gather.19.cloned.1.call-done = bf16[16,128,352]{1,2,0:T(8,128)(2,1)} async-done(((bf16[1,128,352]{1,2,0:T(8,128)(2,1)}), bf16[16,128,352]{1,2,0:T(8,128)(2,1)}) %all-gather.19.cloned.1.call-update) | async-done | bytes 1441808 | tf_op jit(solution)/shard_map/all_gather | solution.py:173
  1027.5 43.5 %all-gather.21.cloned.1.call-done = bf16[16,128,352]{1,2,0:T(8,128)(2,1)} async-done(((bf16[1,128,352]{1,2,0:T(8,128)(2,1)}), bf16[16,128,352]{1,2,0:T(8,128)(2,1)}) %all-gather.21.cloned.1.call-update) | async-done | bytes 1441808 | tf_op jit(solution)/shard_map/all_gather | solution.py:174
  1073.6 43.6 %all-gather.23.cloned.1.call-done = bf16[16,22,2048]{2,1,0:T(8,128)(2,1)} async-done(((bf16[1,22,2048]{2,1,0:T(8,128)(2,1)}), bf16[16,22,2048]{2,1,0:T(8,128)(2,1)}) %all-gather.23.cloned.1.call-update) | async-done | bytes 1441808 | tf_op jit(solution)/shard_map/all_gather | solution.py:175
  (145 shorter events, 72.6 us)
Async XLA Ops:
  7.2 133.8 %reduce-scatter.25.cloned.1.call-start = ((), (), s32[]{:S(2)}) async-start(), calls=%async_computation.16 | async-start | bytes 1114112
  7.9 154.8 %reduce-scatter.27.cloned.1.call-start = ((), (), s32[]{:S(2)}) async-start(), calls=%async_computation.17 | async-start | bytes 1114112
  8.7 229.7 %reduce-scatter.29.cloned.1.call-start = ((), (), s32[]{:S(2)}) async-start(), calls=%async_computation.18 | async-start | bytes 1114112
  9.4 1.4 copy-start.1
  9.4 304.6 %reduce-scatter.31.cloned.1.call-start = ((), (), s32[]{:S(2)}) async-start(), calls=%async_computation.19 | async-start | bytes 1114112
  10.0 379.4 %reduce-scatter.33.cloned.1.call-start = ((), (), s32[]{:S(2)}) async-start(), calls=%async_computation.20 | async-start | bytes 1114112
  10.6 455.8 %reduce-scatter.35.cloned.1.call-start = ((), (), s32[]{:S(2)}) async-start(), calls=%async_computation.21 | async-start | bytes 1531904
  12.6 1.4 copy-start.2
  12.6 530.8 %reduce-scatter.37.cloned.1.call-start = ((), (), s32[]{:S(2)}) async-start(), calls=%async_computation.22 | async-start | bytes 1531904
  15.8 604.2 %reduce-scatter.39.cloned.1.call-start = ((), (), s32[]{:S(2)}) async-start(), calls=%async_computation.23 | async-start | bytes 1671168
  18.5 839.2 %all-gather.11.cloned.1.call-start = ((), (), s32[]{:S(2)}) async-start(), calls=%async_computation.9 | async-start | bytes 1114112 | tf_op jit(solution)/shard_map/all_gather | solution.py:166
  18.7 8.6 copy-start.14
  18.7 8.7 copy-start.15
  18.7 8.8 copy-start.16
  27.7 89.6 %copy-start.13 = (u32[128]{0:T(128)S(1)}, u32[128]{0:T(128)}, u32[]{:S(2)}) copy-start(u32[128]{0:T(128)} %constant.50) | copy-start | bytes 1540
  389.4 1.9 copy-start.10
  389.4 2.6 copy-start.11
  634.1 21.6 %copy-start.12 = (bf16[1,22,2048]{2,1,0:T(8,128)(2,1)S(1)}, bf16[1,22,2048]{2,1,0:T(8,128)(2,1)}, u32[]{:S(2)}) copy-start(bf16[1,22,2048]{2,1,0:T(8,128)(2,1)} %reduce-scatter.39.cloned.1.call-done) | copy-start | bytes 270340
  634.1 21.7 %copy-start.8 = (f32[16,2,8,128]{3,1,2,0:T(2,128)S(1)}, f32[16,2,8,128]{3,1,2,0:T(2,128)}, u32[]{:S(2)}) copy-start(f32[16,2,8,128]{3,1,2,0:T(2,128)} %copy.53) | copy-start | bytes 393220
  634.2 21.7 %copy-start.9 = (f32[16,2,8,128]{3,1,2,0:T(2,128)S(1)}, f32[16,2,8,128]{3,1,2,0:T(2,128)}, u32[]{:S(2)}) copy-start(f32[16,2,8,128]{3,1,2,0:T(2,128)} %copy.54) | copy-start | bytes 393220
  777.8 20.0 %copy-start = (f32[299056]{0:T(1024)S(1)}, f32[299056]{0:T(1024)}, u32[]{:S(2)}) copy-start(f32[299056]{0:T(1024)} %get-tuple-element.39) | copy-start | bytes 3588676
  798.9 89.7 %all-gather.13.cloned.1.call-start = ((), (), s32[]{:S(2)}) async-start(), calls=%async_computation.10 | async-start | bytes 1114112 | tf_op jit(solution)/shard_map/all_gather | solution.py:168
  799.6 134.1 %all-gather.15.cloned.1.call-start = ((), (), s32[]{:S(2)}) async-start(), calls=%async_computation.11 | async-start | bytes 1114112 | tf_op jit(solution)/shard_map/all_gather | solution.py:170
  800.4 178.3 %all-gather.17.cloned.1.call-start = ((), (), s32[]{:S(2)}) async-start(), calls=%async_computation.12 | async-start | bytes 1114112 | tf_op jit(solution)/shard_map/all_gather | solution.py:171
  801.1 223.7 %all-gather.19.cloned.1.call-start = ((), (), s32[]{:S(2)}) async-start(), calls=%async_computation.13 | async-start | bytes 1531904 | tf_op jit(solution)/shard_map/all_gather | solution.py:173
  802.2 268.7 %all-gather.21.cloned.1.call-start = ((), (), s32[]{:S(2)}) async-start(), calls=%async_computation.14 | async-start | bytes 1531904 | tf_op jit(solution)/shard_map/all_gather | solution.py:174
  803.2 314.0 %all-gather.23.cloned.1.call-start = ((), (), s32[]{:S(2)}) async-start(), calls=%async_computation.15 | async-start | bytes 1671168 | tf_op jit(solution)/shard_map/all_gather | solution.py:175
  805.1 52.7 %all-to-all-start = ((bf16[16,1,128,256]{3,2,1,0:T(8,128)(2,1)}), bf16[16,1,128,256]{3,2,1,0:T(8,128)(2,1)S(1)}, u32[]{:S(2)}, u32[]{:S(2)}) async-start(bf16[16,1,128,256]{3,2,1,0:T(8,128)(2,1)} %stack.3), calls=%async_computation | async-start | bytes 2097152 | tf_op jit(solution)/shard_map/all_to_all | solution.py:15
  1073.6 46.0 %copy-start.4 = (bf16[16,128,256]{2,1,0:T(8,128)(2,1)S(1)}, bf16[16,128,256]{2,1,0:T(8,128)(2,1)}, u32[]{:S(2)}) copy-start(bf16[16,128,256]{2,1,0:T(8,128)(2,1)} %all-gather.11.cloned.1.call-done) | copy-start | bytes 3145732
  1120.6 1.6 copy-start.5
  1122.2 1.6 copy-start.6
  1123.8 1.6 copy-start.7
  (1 other events, 1.4 us)
Sparse Core Ops, SparseCore 0:
  11.2 75.6 reduce-scatter.24
  90.4 72.2 reduce-scatter.26
  166.0 72.3 reduce-scatter.28
  241.7 72.2 reduce-scatter.30
  317.1 72.2 reduce-scatter.32
  393.4 72.9 reduce-scatter.34
  470.5 72.8 reduce-scatter.36
  547.0 73.0 reduce-scatter.38
  799.0 44.6 all-gather.10
  846.4 42.1 all-gather.12
  891.6 42.0 all-gather.14
  936.5 42.0 all-gather.16
  981.6 43.1 all-gather.18
  1027.7 43.2 all-gather.20
  1073.8 43.3 all-gather.22
